TPU v7x, 256 devices: a whole 4x4x8 slice. The times are simulated.
256 devices in a mesh: frames: 32 (over z, x_lo, core), runs: 8 (over y, x_hi).
Axes of the slice: x: 4 (x_hi: 2, x_lo: 2; x = x_hi * 2 + x_lo), y: 4, z: 8, core: 2. Of those that a mesh axis runs over, the one named last changes fastest.
Arguments:
- inputs: bfloat16 [8, 131072, 256], P('runs', 'frames'), may hold values from -6 to 6
- first_layer_weight: bfloat16 [3, 256, 256], replicated, may hold values from -0.21875 to 0.21875
- first_layer_bias: bfloat16 [256], replicated, may hold values from -3 to 3
- second_layer_weight: bfloat16 [3, 256, 256], replicated, may hold values from -0.21875 to 0.21875
- second_layer_bias: bfloat16 [256], replicated, may hold values from -3 to 3
- upstream: bfloat16 [8, 131072, 256], P('runs', 'frames'), may hold values from -6 to 6
Outputs:
- outputs: bfloat16 [8, 131072, 256], P('runs', 'frames')
- grad_input: bfloat16 [8, 131072, 256], P('runs', 'frames')
- grad_w_first: float32 [3, 256, 256], replicated
- grad_b_first: float32 [256], replicated
- grad_w_second: float32 [3, 256, 256], replicated
- grad_b_second: float32 [256], replicated
All inputs are finite; a program needn't handle non-finite values.
Results may differ from a plain program's by a relative error of at most 0.007.
Values may be sent and summed in bfloat16 or wider, within the bound.
A program may use at most 128 MiB of HBM per device.

v0:
```python
import math
import jax
import jax.numpy as jnp
from jax import lax
from jax.sharding import PartitionSpec as P

FIRST_SPACING = 256
SECOND_SPACING = 512


def passed_along(block, axis, distance):
    devices = range(lax.axis_size(axis))
    route = [(i - distance, i) for i in devices if i - distance in devices]
    return lax.ppermute(block, axis, route)


def gelu_slope(pre, grad):
    return jax.vjp(jax.nn.gelu, pre)[1](grad)[0]


def causal_conv_apply(extended, weights, bias, dilation, frame_count):
    total = bias.astype(jnp.float32)[None, None, :]
    for k in range(3):
        start = 2 * dilation - k * dilation
        total = total + jnp.einsum(
            "rtc,cd->rtd",
            extended[:, start : start + frame_count],
            weights[k],
            preferred_element_type=jnp.float32,
        )
    return total


def causal_conv_weight_gradient(extended, grad, dilation, frame_count):
    pieces = []
    for k in range(3):
        start = 2 * dilation - k * dilation
        pieces.append(
            jnp.einsum(
                "rtc,rtd->cd",
                extended[:, start : start + frame_count],
                grad,
                preferred_element_type=jnp.float32,
            )
        )
    return jnp.stack(pieces)


def local_terms(grad, weights, dilation, frame_count):
    padded = jnp.pad(grad, ((0, 0), (0, 2 * dilation), (0, 0)))
    total = jnp.zeros(grad.shape, jnp.float32)
    for k in range(3):
        start = k * dilation
        total = total + jnp.einsum(
            "rtd,cd->rtc",
            padded[:, start : start + frame_count],
            weights[k],
            preferred_element_type=jnp.float32,
        )
    return total


def rim_terms(grad, weights, dilation):
    far_terms = jnp.einsum(
        "rtd,cd->rtc", grad[:, : 2 * dilation], weights[2], preferred_element_type=jnp.float32
    )
    near_terms = jnp.einsum(
        "rtd,cd->rtc", grad[:, :dilation], weights[1], preferred_element_type=jnp.float32
    )
    return far_terms + jnp.pad(near_terms, ((0, 0), (dilation, 0), (0, 0)))


def place_tail(arrived, frame_count, dilation):
    return jnp.pad(arrived, ((0, 0), (frame_count - 2 * dilation, 0), (0, 0)))


def causal_conv_input_gradient(grad, weights, dilation, frame_count, layer):
    total = local_terms(grad, weights, dilation, frame_count)
    rim_part = rim_terms(grad, weights, dilation)
    if layer == 2:
        arrived = passed_along(rim_part.astype(jnp.bfloat16), "frames", -1).astype(rim_part.dtype)
    else:
        arrived = passed_along(rim_part.astype(jnp.bfloat16), "frames", -1).astype(rim_part.dtype)
    return total + place_tail(arrived, frame_count, dilation)


def body(
    inputs, first_layer_weight, first_layer_bias, second_layer_weight, second_layer_bias, upstream
):
    frame_count = inputs.shape[1]
    prior_frames = passed_along(inputs[:, frame_count - 2 * FIRST_SPACING :], "frames", 1)
    input_with_history = jnp.concatenate([prior_frames, inputs], axis=1)
    first_preactivation = causal_conv_apply(
        input_with_history, first_layer_weight, first_layer_bias, FIRST_SPACING, frame_count
    )
    hidden_state = (inputs.astype(jnp.float32) + jax.nn.gelu(first_preactivation)).astype(
        jnp.bfloat16
    )
    prior_hidden_frames = passed_along(
        hidden_state[:, frame_count - 2 * SECOND_SPACING :], "frames", 1
    )
    hidden_with_history = jnp.concatenate([prior_hidden_frames, hidden_state], axis=1)
    second_preactivation = causal_conv_apply(
        hidden_with_history, second_layer_weight, second_layer_bias, SECOND_SPACING, frame_count
    )
    result = (hidden_state.astype(jnp.float32) + jax.nn.gelu(second_preactivation)).astype(
        jnp.bfloat16
    )
    output_gradient = upstream.astype(jnp.float32)
    second_layer_gradient = gelu_slope(second_preactivation, output_gradient).astype(jnp.bfloat16)
    second_weight_delta = causal_conv_weight_gradient(
        hidden_with_history, second_layer_gradient, SECOND_SPACING, frame_count
    )
    db_second = jnp.sum(second_layer_gradient.astype(jnp.float32), axis=(0, 1))
    hidden_gradient = output_gradient + causal_conv_input_gradient(
        second_layer_gradient, second_layer_weight, SECOND_SPACING, frame_count, 2
    )
    first_layer_gradient = gelu_slope(first_preactivation, hidden_gradient).astype(jnp.bfloat16)
    input_gradient_rows = (
        hidden_gradient
        + causal_conv_input_gradient(
            first_layer_gradient, first_layer_weight, FIRST_SPACING, frame_count, 1
        )
    ).astype(jnp.bfloat16)
    first_weight_delta = causal_conv_weight_gradient(
        input_with_history, first_layer_gradient, FIRST_SPACING, frame_count
    )
    db_first = jnp.sum(first_layer_gradient.astype(jnp.float32), axis=(0, 1))
    factor = 1.0 / math.sqrt(
        inputs.shape[0] * lax.axis_size("runs") * frame_count * lax.axis_size("frames")
    )
    sum_w_first, sum_b_first, sum_w_second, sum_b_second = lax.psum(
        (first_weight_delta, db_first, second_weight_delta, db_second), ("frames", "runs")
    )
    sum_w_first = sum_w_first * factor
    sum_b_first = sum_b_first * factor
    sum_w_second = sum_w_second * factor
    sum_b_second = sum_b_second * factor
    return (result, input_gradient_rows, sum_w_first, sum_b_first, sum_w_second, sum_b_second)


def solution(mesh):
    return jax.shard_map(
        body,
        mesh=mesh,
        in_specs=(P("runs", "frames", None), P(), P(), P(), P(), P("runs", "frames", None)),
        out_specs=(P("runs", "frames", None), P("runs", "frames", None), P(), P(), P(), P()),
        check_vma=False,
    )
```

profile of v0, /device:TPU:2, one launch (start us, length us, event | category | flops | bytes accessed | tf_op | source)
XLA Modules:
  0.0 347.0 jit_solution(14924929035905152933)
XLA Ops:
  7.2 0.0 all-reduce.10.cloned.1.call-start
  7.2 1.0 slice.77
  8.2 1.9 collective-permute-start
  10.1 0.7 convert_element_type.57
  10.8 0.0 copy-start
  10.8 2.5 convolution_add_fusion.9
  13.2 0.0 copy-start.1
  13.2 2.6 collective-permute-done
  15.9 0.0 copy-done
  15.9 0.1 constant_dynamic-update-slice_fusion
  16.1 0.0 copy-done.1
  16.1 0.7 convolution_add_fusion.8
  16.8 0.0 copy-start.4
  16.8 0.0 copy-start.3
  16.8 1.9 fusion.24
  18.8 2.1 collective-permute-start.1
  20.9 0.0 copy-done.4
  20.9 0.0 copy-done.3
  20.9 0.7 convolution_add_fusion.6
  21.6 0.0 copy-start.2
  21.6 7.7 %collective-permute-done.1 = bf16[1,1024,256]{2,1,0:T(8,128)(2,1)S(1)} collective-permute-done((bf16[1,1024,256]{2,1,0:T(8,128)(2,1)S(1)}, bf16[1,1024,256]{2,1,0:T(8,128)(2,1)S(1)}, u32[]{:S(2)}, u32[]{:S(2)}) %collective-permute-start.1) | collective-permute-done | bytes 524320 | tf_op jit(solution)/shard_map/ppermute | solution.py:14
  29.3 0.8 convolution_add_fusion.5
  30.1 0.0 copy-done.2
  30.1 7.2 %convert_reduce_fusion = (f32[256]{0:T(256)S(1)}, bf16[1,4096,256]{2,1,0:T(8,128)(2,1)S(1)}, bf16[1,4096,256]{2,1,0:T(8,128)(2,1)}) fusion(bf16[1,4096,256]{2,1,0:T(8,128)(2,1)S(1)} %copy-done.2, bf16[1,4096,256]{2,1,0:T(8,128)(2,1)S(1)} %get-tuple-element.21, f32[4096,256]{1,0:T(8,128)S(1)} %convolution_add_fusion.5, ...), kind=kOutput, calls=%fused_computation.47 | convolution fusion | flops 570425088 | bytes 15336448 | tf_op jit(solution)/shard_map/rtc,cd->rtd/dot_general | solution.py:25
  37.3 1.0 fusion.62
  38.3 0.2 convolution_bitcast_fusion.2
  38.5 0.7 fusion.52
  39.3 0.3 fusion.59
  39.6 2.1 collective-permute-start.2
  41.7 1.0 fusion.67
  42.7 1.0 fusion.70
  43.6 0.9 pad_maximum_fusion.2
  44.6 0.8 convolution_add_fusion.3
  45.3 2.9 collective-permute-done.2
  48.2 6.9 %convert_reduce_fusion.1 = (f32[256]{0:T(256)S(1)}, bf16[1,4096,256]{2,1,0:T(8,128)(2,1)S(1)}, f32[1,4096,256]{2,1,0:T(8,128)}) fusion(f32[4096,256]{1,0:T(8,128)S(1)} %get-tuple-element.22, bf16[1,1024,256]{2,1,0:T(8,128)(2,1)S(1)} %collective-permute-done.2, bf16[1,4096,256]{2,1,0:T(8,128)(2,1)S(1)} %copy-done.2, ...), kind=kOutput, calls=%fused_computation.48 | convolution fusion | flops 565182208 | bytes 19530752 | tf_op jit(solution)/shard_map/rtd,cd->rtc/dot_general | solution.py:54
  55.1 1.0 fusion.78
  56.1 1.0 fusion.81
  57.1 0.8 fusion.73
  57.9 0.2 convolution_bitcast_fusion.3
  58.1 0.7 fusion.44
  58.8 0.3 fusion.61
  59.1 3.8 %collective-permute-start.3 = (bf16[1,512,256]{2,1,0:T(8,128)(2,1)S(1)}, bf16[1,512,256]{2,1,0:T(8,128)(2,1)S(1)}, u32[]{:S(2)}, u32[]{:S(2)}) collective-permute-start(bf16[1,512,256]{2,1,0:T(8,128)(2,1)S(1)} %fusion.61), channel_id=1, source_target_pairs={{8,0},{16,8},{24,16},{32,24},{40,32},{48,40},{56,48},{64,56},{72,6... | collective-permute-start | bytes 786440 | tf_op jit(solution)/shard_map/ppermute | solution.py:14
  62.9 2.8 convolution_add_fusion.1
  65.7 0.9 pad_maximum_fusion.1
  66.6 0.0 all-reduce.10.cloned.1.call-update
  66.6 82.8 %all-reduce.6 = (f32[256]{0:T(256)S(1)}, f32[256]{0:T(256)S(1)}) all-reduce(f32[256]{0:T(256)S(1)} %get-tuple-element.18, f32[256]{0:T(256)S(1)} %get-tuple-element.16), channel_id=1, replica_groups=mesh['frames'=32,'runs'=8] {'frames','runs'}, use_global_device_ids=true, to_apply=%region_2.3 | all-reduce | flops 512 | bytes 4096 | tf_op jit(solution)/shard_map/psum | solution.py:132
  149.4 0.6 broadcast_multiply_fusion.2
  150.0 0.0 collective-permute-done.3
  150.0 8.1 %add_convert_fusion = bf16[1,4096,256]{2,1,0:T(8,128)(2,1)} fusion(f32[4096,256]{1,0:T(8,128)} %convolution_add_fusion.1, bf16[1,4096,256]{2,1,0:T(8,128)(2,1)S(1)} %get-tuple-element.19, bf16[1,512,256]{2,1,0:T(8,128)(2,1)S(1)} %collective-permute-done.3, f32[1,4096,256]{2,1,0:T(8,128)} %get-tuple-element.23, ...), kind=kOutput, calls=%fused_computation.49 | convolution fusion | flops 546308096 | bytes 15597568 | tf_op jit(solution)/shard_map/rtd,cd->rtc/dot_general | solution.py:54
  158.1 178.3 %all-reduce.10.cloned.1.call-done = (f32[3,256,256]{1,2,0:T(8,128)}, f32[3,256,256]{1,2,0:T(8,128)}) async-done(((f32[3,256,256]{1,2,0:T(8,128)}, f32[3,256,256]{1,2,0:T(8,128)}), (f32[3,256,256]{1,2,0:T(8,128)}, f32[3,256,256]{1,2,0:T(8,128)})) %all-reduce.10.cloned.1.call-update) | async-done | bytes 1572880 | tf_op jit(solution)/shard_map/psum | solution.py:132
  336.4 1.5 broadcast_multiply_fusion
  337.8 1.1 copy.18
  339.0 1.1 copy.17
  (3 shorter events, 0.1 us)
Async XLA Ops:
  7.2 329.2 %all-reduce.10.cloned.1.call-start = ((), (), s32[]{:S(2)}) async-start(), calls=%async_computation | async-start | bytes 3145728 | tf_op jit(solution)/shard_map/psum | solution.py:132
  8.2 7.7 %collective-permute-start = (bf16[1,512,256]{2,1,0:T(8,128)(2,1)S(1)}, bf16[1,512,256]{2,1,0:T(8,128)(2,1)S(1)}, u32[]{:S(2)}, u32[]{:S(2)}) collective-permute-start(bf16[1,512,256]{2,1,0:T(8,128)(2,1)S(1)} %slice.77), channel_id=1, source_target_pairs={{0,8},{8,16},{16,24},{24,32},{32,40},{40,48},{48,56},{56,64},{64,7... | collective-permute-start | bytes 786440 | tf_op jit(solution)/shard_map/ppermute | solution.py:14
  10.8 5.1 %copy-start = (bf16[1,4096,256]{2,1,0:T(8,128)(2,1)S(1)}, bf16[1,4096,256]{2,1,0:T(8,128)(2,1)}, u32[]{:S(2)}) copy-start(bf16[1,4096,256]{2,1,0:T(8,128)(2,1)} %param.6) | copy-start | bytes 6291460
  13.2 2.8 copy-start.1
  16.8 4.1 %copy-start.4 = (bf16[256]{0:T(256)(128)(2,1)S(1)}, bf16[256]{0:T(256)(128)(2,1)}, u32[]{:S(2)}) copy-start(bf16[256]{0:T(256)(128)(2,1)} %param.10) | copy-start | bytes 1540
  16.8 4.1 %copy-start.3 = (bf16[3,256,256]{2,1,0:T(8,128)(2,1)S(1)}, bf16[3,256,256]{2,1,0:T(8,128)(2,1)}, u32[]{:S(2)}) copy-start(bf16[3,256,256]{2,1,0:T(8,128)(2,1)} %param.9) | copy-start | bytes 1179652
  18.8 10.5 %collective-permute-start.1 = (bf16[1,1024,256]{2,1,0:T(8,128)(2,1)S(1)}, bf16[1,1024,256]{2,1,0:T(8,128)(2,1)S(1)}, u32[]{:S(2)}, u32[]{:S(2)}) collective-permute-start(bf16[1,1024,256]{2,1,0:T(8,128)(2,1)S(1)} %slice.98), channel_id=1, source_target_pairs={{0,8},{8,16},{16,24},{24,32},{32,40},{40,48},{48,56},{56,64},{64,7... | collective-permute-start | bytes 1572872 | tf_op jit(solution)/shard_map/ppermute | solution.py:14
  21.6 8.4 %copy-start.2 = (bf16[1,4096,256]{2,1,0:T(8,128)(2,1)S(1)}, bf16[1,4096,256]{2,1,0:T(8,128)(2,1)}, u32[]{:S(2)}) copy-start(bf16[1,4096,256]{2,1,0:T(8,128)(2,1)} %param.11) | copy-start | bytes 6291460
  39.6 8.6 %collective-permute-start.2 = (bf16[1,1024,256]{2,1,0:T(8,128)(2,1)S(1)}, bf16[1,1024,256]{2,1,0:T(8,128)(2,1)S(1)}, u32[]{:S(2)}, u32[]{:S(2)}) collective-permute-start(bf16[1,1024,256]{2,1,0:T(8,128)(2,1)S(1)} %fusion.59), channel_id=1, source_target_pairs={{8,0},{16,8},{24,16},{32,24},{40,32},{48,40},{56,48},{64,56},{72,6... | collective-permute-start | bytes 1572872 | tf_op jit(solution)/shard_map/ppermute | solution.py:14
  59.1 90.9 %collective-permute-start.3 = (bf16[1,512,256]{2,1,0:T(8,128)(2,1)S(1)}, bf16[1,512,256]{2,1,0:T(8,128)(2,1)S(1)}, u32[]{:S(2)}, u32[]{:S(2)}) collective-permute-start(bf16[1,512,256]{2,1,0:T(8,128)(2,1)S(1)} %fusion.61), channel_id=1, source_target_pairs={{8,0},{16,8},{24,16},{32,24},{40,32},{48,40},{56,48},{64,56},{72,6... | collective-permute-start | bytes 786440 | tf_op jit(solution)/shard_map/ppermute | solution.py:14
Sparse Core Ops, SparseCore 0:
  66.7 269.5 all-reduce.9
where the time goes:
time: 347 us
  waiting for transfers between devices  191 us (55%)
  blocking collectives  82.8 us (24%)
  matrix products  40.5 us (12%)
  between operations  14.3 us (4%)
  starting transfers between devices  9.95 us (3%)
  other arithmetic  4.58 us (1%)
  local copies, waits for them, and re-layouts  3.49 us (1%)
    psum x1, waiting for transfers between devices, body(): lax.psum((first_weight_delta, db_first, second_weight_delta, db_second),...  178 us
    psum x1, blocking collectives, body(): lax.psum((first_weight_delta, db_first, second_weight_delta, db_second),...  82.8 us
    dot_general x6, matrix products, local_terms(): jnp.einsum('rtd,cd->rtc', padded[:, start:start + frame_count], weights[k...  20 us
    dot_general x6, matrix products, causal_conv_apply(): jnp.einsum('rtc,cd->rtd', extended[:, start:start + frame_count], weights...  13.8 us
    ppermute x4, waiting for transfers between devices, passed_along(): return lax.ppermute(block, axis, route)  13.1 us
    ppermute x4, starting transfers between devices, passed_along(): return lax.ppermute(block, axis, route)  9.91 us
  transfers between devices with their start and end apart: 5, of which 4 were waited for; matrix products, arithmetic and copies ran while one was open for 6% of the time, Pallas kernels for 0%

commit v1 on v0

--- a/solution.py
+++ b/solution.py
@@ -129,8 +129,9 @@
     factor = 1.0 / math.sqrt(
         inputs.shape[0] * lax.axis_size("runs") * frame_count * lax.axis_size("frames")
     )
-    sum_w_first, sum_b_first, sum_w_second, sum_b_second = lax.psum(
-        (first_weight_delta, db_first, second_weight_delta, db_second), ("frames", "runs")
+    sum_w_first, sum_b_first, sum_w_second, sum_b_second = jax.lax.psum(
+        jax.lax.psum((first_weight_delta, db_first, second_weight_delta, db_second), "runs"),
+        "frames",
     )
     sum_w_first = sum_w_first * factor
     sum_b_first = sum_b_first * factor

time: 347 us -> 412 us (1.19); the launches traced: 347 us -> 407 us
  waiting for transfers between devices: 191 us -> 262 us
  blocking collectives: 82.8 us -> 72.2 us
    psum x1 -> x2, waiting for transfers between devices: 178 us -> 249 us  [the longest x1 144 us: body(): jax.lax.psum(jax.lax.psum((first_weight_delta, db_first, second_weight_de...]
    psum x1 -> x2, blocking collectives: 82.8 us -> 72.2 us  [the longest x1 50.1 us: body(): jax.lax.psum(jax.lax.psum((first_weight_delta, db_first, second_weight_de...]
  transfers between devices with their start and end apart: 5 -> 6, of which waited for: 4 -> 5; matrix products, arithmetic and copies ran while one was open for 6% -> 5% of each run, Pallas kernels for 0% -> 0%
where the time goes in v1:
time: 412 us; the launch traced here: 407 us
  waiting for transfers between devices  262 us (64%)
  blocking collectives  72.2 us (18%)
  matrix products  40.5 us (10%)
  between operations  14.3 us (3%)
  starting transfers between devices  9.99 us (2%)
  other arithmetic  4.63 us (1%)
    psum x1, waiting for transfers between devices, body(): jax.lax.psum(jax.lax.psum((first_weight_delta, db_first, second_weight_de...  144 us
    psum x1, waiting for transfers between devices, body(): jax.lax.psum((first_weight_delta, db_first, second_weight_delta, db_secon...  104 us
    psum x1, blocking collectives, body(): jax.lax.psum(jax.lax.psum((first_weight_delta, db_first, second_weight_de...  50.1 us
    psum x1, blocking collectives, body(): jax.lax.psum((first_weight_delta, db_first, second_weight_delta, db_secon...  22.1 us
    dot_general x6, matrix products, local_terms(): jnp.einsum('rtd,cd->rtc', padded[:, start:start + frame_count], weights[k...  20 us
    dot_general x6, matrix products, causal_conv_apply(): jnp.einsum('rtc,cd->rtd', extended[:, start:start + frame_count], weights...  13.8 us
    ppermute x4, waiting for transfers between devices, passed_along(): return lax.ppermute(block, axis, route)  13.2 us
    ppermute x4, starting transfers between devices, passed_along(): return lax.ppermute(block, axis, route)  9.91 us
  transfers between devices with their start and end apart: 6, of which 5 were waited for; matrix products, arithmetic and copies ran while one was open for 5% of the time, Pallas kernels for 0%

profile of v1, /device:TPU:2, one launch (start us, length us, event | category | flops | bytes accessed | tf_op | source)
XLA Modules:
  0.0 406.9 jit_solution(17970216004452377093)
XLA Ops:
  7.2 0.0 all-reduce.15.cloned.1.call-start
  7.2 1.0 slice.77
  8.2 1.9 collective-permute-start
  10.1 0.7 convert_element_type.57
  10.8 0.0 copy-start
  10.8 2.5 convolution_add_fusion.9
  13.2 0.0 copy-start.1
  13.2 2.6 collective-permute-done
  15.9 0.0 copy-done
  15.9 0.1 constant_dynamic-update-slice_fusion
  16.1 0.0 copy-done.1
  16.1 0.7 convolution_add_fusion.8
  16.8 0.0 copy-start.4
  16.8 0.0 copy-start.3
  16.8 2.0 fusion.24
  18.8 2.1 collective-permute-start.1
  20.9 0.0 copy-done.4
  20.9 0.0 copy-done.3
  20.9 0.7 convolution_add_fusion.6
  21.6 0.0 copy-start.2
  21.7 7.7 %collective-permute-done.1 = bf16[1,1024,256]{2,1,0:T(8,128)(2,1)S(1)} collective-permute-done((bf16[1,1024,256]{2,1,0:T(8,128)(2,1)S(1)}, bf16[1,1024,256]{2,1,0:T(8,128)(2,1)S(1)}, u32[]{:S(2)}, u32[]{:S(2)}) %collective-permute-start.1) | collective-permute-done | bytes 524320 | tf_op jit(solution)/shard_map/ppermute | solution.py:14
  29.3 0.8 convolution_add_fusion.5
  30.1 0.0 copy-done.2
  30.1 7.2 %convert_reduce_fusion = (f32[256]{0:T(256)S(1)}, bf16[1,4096,256]{2,1,0:T(8,128)(2,1)S(1)}, bf16[1,4096,256]{2,1,0:T(8,128)(2,1)}) fusion(bf16[1,4096,256]{2,1,0:T(8,128)(2,1)S(1)} %copy-done.2, bf16[1,4096,256]{2,1,0:T(8,128)(2,1)S(1)} %get-tuple-element.25, f32[4096,256]{1,0:T(8,128)S(1)} %convolution_add_fusion.5, ...), kind=kOutput, calls=%fused_computation.47 | convolution fusion | flops 570425088 | bytes 15336448 | tf_op jit(solution)/shard_map/rtc,cd->rtd/dot_general | solution.py:25
  37.3 1.0 fusion.62
  38.3 0.2 convolution_bitcast_fusion.2
  38.5 0.7 fusion.52
  39.3 0.3 fusion.59
  39.6 2.1 collective-permute-start.2
  41.7 1.0 fusion.67
  42.7 1.0 fusion.70
  43.7 0.9 pad_maximum_fusion.2
  44.6 0.8 convolution_add_fusion.3
  45.4 2.9 collective-permute-done.2
  48.2 6.9 %convert_reduce_fusion.1 = (f32[256]{0:T(256)S(1)}, bf16[1,4096,256]{2,1,0:T(8,128)(2,1)S(1)}, f32[1,4096,256]{2,1,0:T(8,128)}) fusion(f32[4096,256]{1,0:T(8,128)S(1)} %get-tuple-element.26, bf16[1,1024,256]{2,1,0:T(8,128)(2,1)S(1)} %collective-permute-done.2, bf16[1,4096,256]{2,1,0:T(8,128)(2,1)S(1)} %copy-done.2, ...), kind=kOutput, calls=%fused_computation.48 | convolution fusion | flops 565182208 | bytes 19530752 | tf_op jit(solution)/shard_map/rtd,cd->rtc/dot_general | solution.py:54
  55.1 1.0 fusion.78
  56.1 1.0 fusion.81
  57.1 0.8 fusion.73
  57.9 0.9 pad_maximum_fusion.1
  58.8 0.0 all-reduce.15.cloned.1.call-update
  58.8 0.0 all-reduce.13.cloned.1.call-start
  58.9 0.2 convolution_bitcast_fusion.3
  59.1 0.3 fusion.61
  59.4 3.8 collective-permute-start.3
  63.2 104.5 %all-reduce.15.cloned.1.call-done = (f32[3,256,256]{1,2,0:T(8,128)}, f32[3,256,256]{1,2,0:T(8,128)}) async-done(((f32[3,256,256]{1,2,0:T(8,128)}, f32[3,256,256]{1,2,0:T(8,128)}), (f32[3,256,256]{1,2,0:T(8,128)}, f32[3,256,256]{1,2,0:T(8,128)})) %all-reduce.15.cloned.1.call-update) | async-done | bytes 1572880 | tf_op jit(solution)/shard_map/psum | solution.py:133
  167.7 0.0 all-reduce.13.cloned.1.call-update
  167.7 0.7 fusion.44
  168.4 2.8 convolution_add_fusion.1
  171.2 22.1 %all-reduce.8 = (f32[256]{0:T(256)S(1)}, f32[256]{0:T(256)S(1)}) all-reduce(f32[256]{0:T(256)S(1)} %get-tuple-element.22, f32[256]{0:T(256)S(1)} %get-tuple-element.20), channel_id=1, replica_groups=mesh['frames'=32,'runs'=8] {'runs'}, use_global_device_ids=true, to_apply=%region_3.4 | all-reduce | flops 512 | bytes 4096 | tf_op jit(solution)/shard_map/psum | solution.py:133
  193.3 50.1 %all-reduce.6 = (f32[256]{0:T(256)S(1)}, f32[256]{0:T(256)S(1)}) all-reduce(f32[256]{0:T(256)S(1)} %get-tuple-element.16, f32[256]{0:T(256)S(1)} %get-tuple-element.17), channel_id=1, replica_groups=mesh['frames'=32,'runs'=8] {'frames'}, use_global_device_ids=true, to_apply=%region_4.5 | all-reduce | flops 512 | bytes 4096 | tf_op jit(solution)/shard_map/psum | solution.py:132
  243.4 0.6 broadcast_multiply_fusion.2
  244.0 0.0 collective-permute-done.3
  244.0 8.1 %add_convert_fusion = bf16[1,4096,256]{2,1,0:T(8,128)(2,1)} fusion(f32[4096,256]{1,0:T(8,128)} %convolution_add_fusion.1, bf16[1,4096,256]{2,1,0:T(8,128)(2,1)S(1)} %get-tuple-element.23, bf16[1,512,256]{2,1,0:T(8,128)(2,1)S(1)} %collective-permute-done.3, f32[1,4096,256]{2,1,0:T(8,128)} %get-tuple-element.27, ...), kind=kOutput, calls=%fused_computation.49 | convolution fusion | flops 546308096 | bytes 15597568 | tf_op jit(solution)/shard_map/rtd,cd->rtc/dot_general | solution.py:54
  252.1 144.2 %all-reduce.13.cloned.1.call-done = (f32[3,256,256]{1,2,0:T(8,128)}, f32[3,256,256]{1,2,0:T(8,128)}) async-done(((f32[3,256,256]{1,2,0:T(8,128)}, f32[3,256,256]{1,2,0:T(8,128)}), (f32[3,256,256]{1,2,0:T(8,128)}, f32[3,256,256]{1,2,0:T(8,128)})) %all-reduce.13.cloned.1.call-update) | async-done | bytes 1572880 | tf_op jit(solution)/shard_map/psum | solution.py:132
  396.3 1.5 broadcast_multiply_fusion
  397.8 1.2 copy.18
  398.9 1.1 copy.17
  (3 shorter events, 0.1 us)
Async XLA Ops:
  7.2 160.5 %all-reduce.15.cloned.1.call-start = ((), (), s32[]{:S(2)}) async-start(), calls=%async_computation.1 | async-start | bytes 3145728 | tf_op jit(solution)/shard_map/psum | solution.py:133
  8.2 7.7 %collective-permute-start = (bf16[1,512,256]{2,1,0:T(8,128)(2,1)S(1)}, bf16[1,512,256]{2,1,0:T(8,128)(2,1)S(1)}, u32[]{:S(2)}, u32[]{:S(2)}) collective-permute-start(bf16[1,512,256]{2,1,0:T(8,128)(2,1)S(1)} %slice.77), channel_id=1, source_target_pairs={{0,8},{8,16},{16,24},{24,32},{32,40},{40,48},{48,56},{56,64},{64,7... | collective-permute-start | bytes 786440 | tf_op jit(solution)/shard_map/ppermute | solution.py:14
  10.8 5.1 %copy-start = (bf16[1,4096,256]{2,1,0:T(8,128)(2,1)S(1)}, bf16[1,4096,256]{2,1,0:T(8,128)(2,1)}, u32[]{:S(2)}) copy-start(bf16[1,4096,256]{2,1,0:T(8,128)(2,1)} %param.6) | copy-start | bytes 6291460
  13.2 2.8 copy-start.1
  16.8 4.1 %copy-start.4 = (bf16[256]{0:T(256)(128)(2,1)S(1)}, bf16[256]{0:T(256)(128)(2,1)}, u32[]{:S(2)}) copy-start(bf16[256]{0:T(256)(128)(2,1)} %param.10) | copy-start | bytes 1540
  16.8 4.1 %copy-start.3 = (bf16[3,256,256]{2,1,0:T(8,128)(2,1)S(1)}, bf16[3,256,256]{2,1,0:T(8,128)(2,1)}, u32[]{:S(2)}) copy-start(bf16[3,256,256]{2,1,0:T(8,128)(2,1)} %param.9) | copy-start | bytes 1179652
  18.8 10.5 %collective-permute-start.1 = (bf16[1,1024,256]{2,1,0:T(8,128)(2,1)S(1)}, bf16[1,1024,256]{2,1,0:T(8,128)(2,1)S(1)}, u32[]{:S(2)}, u32[]{:S(2)}) collective-permute-start(bf16[1,1024,256]{2,1,0:T(8,128)(2,1)S(1)} %slice.98), channel_id=1, source_target_pairs={{0,8},{8,16},{16,24},{24,32},{32,40},{40,48},{48,56},{56,64},{64,7... | collective-permute-start | bytes 1572872 | tf_op jit(solution)/shard_map/ppermute | solution.py:14
  21.6 8.5 %copy-start.2 = (bf16[1,4096,256]{2,1,0:T(8,128)(2,1)S(1)}, bf16[1,4096,256]{2,1,0:T(8,128)(2,1)}, u32[]{:S(2)}) copy-start(bf16[1,4096,256]{2,1,0:T(8,128)(2,1)} %param.11) | copy-start | bytes 6291460
  39.6 8.6 %collective-permute-start.2 = (bf16[1,1024,256]{2,1,0:T(8,128)(2,1)S(1)}, bf16[1,1024,256]{2,1,0:T(8,128)(2,1)S(1)}, u32[]{:S(2)}, u32[]{:S(2)}) collective-permute-start(bf16[1,1024,256]{2,1,0:T(8,128)(2,1)S(1)} %fusion.59), channel_id=1, source_target_pairs={{8,0},{16,8},{24,16},{32,24},{40,32},{48,40},{56,48},{64,56},{72,6... | collective-permute-start | bytes 1572872 | tf_op jit(solution)/shard_map/ppermute | solution.py:14
  58.8 337.4 %all-reduce.13.cloned.1.call-start = ((), (), s32[]{:S(2)}) async-start(), calls=%async_computation | async-start | bytes 3145728 | tf_op jit(solution)/shard_map/psum | solution.py:132
  59.4 184.6 %collective-permute-start.3 = (bf16[1,512,256]{2,1,0:T(8,128)(2,1)S(1)}, bf16[1,512,256]{2,1,0:T(8,128)(2,1)S(1)}, u32[]{:S(2)}, u32[]{:S(2)}) collective-permute-start(bf16[1,512,256]{2,1,0:T(8,128)(2,1)S(1)} %fusion.61), channel_id=1, source_target_pairs={{8,0},{16,8},{24,16},{32,24},{40,32},{48,40},{56,48},{64,56},{72,6... | collective-permute-start | bytes 786440 | tf_op jit(solution)/shard_map/ppermute | solution.py:14
Sparse Core Ops, SparseCore 0:
  59.0 108.6 all-reduce.14
  170.3 225.8 all-reduce.12
